TPU v7x, 1024 devices: a whole 8x8x8 slice. The times are simulated.
1024 devices in a mesh: node: 64 (over x, z), local: 16 (over y, core).
Axes of the slice: x: 8, y: 8, z: 8, core: 2. Of those that a mesh axis runs over, the one named last changes fastest.
Arguments:
- grad_out: bfloat16 [8192, 6144], P('node', 'local'), may hold values from -6 to 6
- gate_prob: float32 [8192, 8], P('node'), may hold values from 0.05 to 0.5
- routes: int32 [8192, 8], P('node'), may hold values from 0 to 63, all different within a row; in each aligned block of 128 rows (0 to 127, 128 to 255, ...) at most 16 rows name the same one
- paired: int32 [32], replicated, may hold values from 0 to 1, as said below
- saved_pre: bfloat16 [64, 64, 16, 2, 1024], P('node'), may hold values from -6 to 6
- w_gate: bfloat16 [64, 6144, 1024], P('node', 'local'), may hold values from -0.078125 to 0.078125
- w_up: bfloat16 [64, 6144, 1024], P('node', 'local'), may hold values from -0.078125 to 0.078125
- w_down: bfloat16 [64, 1024, 6144], P('node', None, 'local'), may hold values from -0.1875 to 0.1875
Outputs:
- grad_in: bfloat16 [8192, 6144], P('node', 'local')
- grad_down: bfloat16 [64, 1024, 6144], P('node', None, 'local')
Inputs may be any that keep to these rules, and one draw needn't show every extreme that they name: `routes`: each token names 8 different slots. Within the 128 tokens of one block (one index of node), no slot is named by more than 16 tokens, a bound that some block reaches. Exactly half of the pairs are paired, which ones drawn from the seed.
All inputs are finite; a program needn't handle non-finite values.
Results may differ from a plain program's by a relative error of at most 0.023.
Values may be sent and summed in bfloat16 or wider, within the bound.
A program may use at most 64 MiB of HBM per device.

v0:
```python
import jax
import jax.numpy as jnp
from jax import lax
from jax.sharding import PartitionSpec as P


def partner_2(block, axis, apart):
    count = lax.axis_size(axis)
    route = []
    for low in range(count):
        high = low | 1 << apart
        if high != low and high < count:
            route += [(low, high), (high, low)]
    return lax.ppermute(block, axis, route)


def swiglu_grads(dhid, pre):
    gval = pre[:, 0, :].astype(jnp.float32)
    uval = pre[:, 1, :].astype(jnp.float32)
    sigm = jax.nn.sigmoid(gval)
    dgate = (dhid * uval * sigm * (1.0 + gval * (1.0 - sigm))).astype(jnp.bfloat16)
    dup = (dhid * gval * sigm).astype(jnp.bfloat16)
    return (dgate, dup)


def activation(pre):
    gval = pre[:, 0, :].astype(jnp.float32)
    uval = pre[:, 1, :].astype(jnp.float32)
    return (gval * jax.nn.sigmoid(gval) * uval).astype(jnp.bfloat16)


def body(grad_out, gate_prob, routes, paired, saved_pre, w_gate, w_up, w_down):
    tok_rows, part_slice = grad_out.shape
    nodes = lax.axis_size("node")
    worker_count = lax.axis_size("local")
    top_count = routes.shape[1]
    capacity = saved_pre.shape[2]
    hidden = saved_pre.shape[4]
    rows_per_slot = nodes * capacity
    pair_count = tok_rows * top_count
    flat_routes = routes.reshape(-1)
    onehot = (flat_routes[:, None] == jnp.arange(nodes, dtype=jnp.int32)[None, :]).astype(jnp.int32)
    before = jnp.cumsum(onehot, axis=0) - onehot
    row_rank = jnp.sum(before * onehot, axis=1)
    target = flat_routes * capacity + row_rank
    source_of = (
        jnp.full((rows_per_slot,), pair_count, jnp.int32)
        .at[target]
        .set(jnp.arange(pair_count, dtype=jnp.int32))
    )
    gated = (grad_out.astype(jnp.float32)[:, None, :] * gate_prob[:, :, None]).astype(jnp.bfloat16)
    gated = jnp.concatenate(
        [gated.reshape(pair_count, part_slice), jnp.zeros((1, part_slice), jnp.bfloat16)], axis=0
    )
    outgoing = jnp.take(gated, source_of, axis=0)
    arrived = lax.all_to_all(
        outgoing.reshape(nodes, capacity, part_slice),
        "node",
        split_axis=0,
        concat_axis=0,
        tiled=True,
    )
    token_rows = arrived.reshape(rows_per_slot, part_slice)
    partial_value = lax.dot_general(
        token_rows, w_down[0], (((1,), (1,)), ((), ())), preferred_element_type=jnp.float32
    )
    partial_value = lax.optimization_barrier(partial_value.astype(jnp.bfloat16)).astype(jnp.float32)
    saved_rows = saved_pre[0].reshape(rows_per_slot, 2, hidden)
    act = activation(saved_rows)
    share = rows_per_slot // worker_count
    dhid = lax.psum_scatter(
        partial_value.astype(jnp.bfloat16), "local", scatter_dimension=0, tiled=True
    ).astype(jnp.float32)
    start = lax.axis_index("local") * share
    pre_share = lax.dynamic_slice_in_dim(saved_rows, start, share, 0)
    dgate, dup = swiglu_grads(dhid, pre_share)
    dgate, dup = (
        lax.all_gather(dgate, "local", axis=0, tiled=True),
        lax.all_gather(dup, "local", axis=0, tiled=True),
    )
    contract = (((1,), (1,)), ((), ()))
    back = lax.dot_general(dgate, w_gate[0], contract, preferred_element_type=jnp.float32)
    back = back + lax.dot_general(dup, w_up[0], contract, preferred_element_type=jnp.float32)
    back = back.astype(jnp.bfloat16)
    own = lax.dot_general(
        act, token_rows, (((0,), (0,)), ((), ())), preferred_element_type=jnp.float32
    ).astype(jnp.bfloat16)
    homing = lax.all_to_all(
        back.reshape(nodes, capacity, part_slice), "node", split_axis=0, concat_axis=0, tiled=True
    )
    picked = jnp.take(homing.reshape(rows_per_slot, part_slice), target, axis=0)
    grad_in = jnp.sum(
        picked.reshape(tok_rows, top_count, part_slice).astype(jnp.float32), axis=1
    ).astype(jnp.bfloat16)
    top_bit = nodes.bit_length() - 2
    partner = partner_2(own, "node", top_bit)
    half = nodes // 2
    my_pair = lax.axis_index("node") % half
    flag = jnp.sum(
        paired.astype(jnp.float32)
        * (jnp.arange(half, dtype=jnp.int32) == my_pair).astype(jnp.float32)
    )
    own_f = lax.optimization_barrier(own).astype(jnp.float32)
    grad_down = (own_f + flag * partner.astype(jnp.float32)).astype(jnp.bfloat16)
    return (grad_in, grad_down[None])


def solution(mesh):
    in_specs = (
        P("node", "local"),
        P("node", None),
        P("node", None),
        P(),
        P("node", None, None, None, None),
        P("node", "local", None),
        P("node", "local", None),
        P("node", None, "local"),
    )
    out_specs = (P("node", "local"), P("node", None, "local"))
    return jax.shard_map(body, mesh=mesh, in_specs=in_specs, out_specs=out_specs, check_vma=False)
```

profile of v0, /device:TPU:16, one launch (start us, length us, event | category | flops | bytes accessed | tf_op | source)
XLA Modules:
  0.0 327.8 jit_solution(2058825531278344453)
XLA Ops:
  7.2 0.0 copy-start
  7.2 0.0 copy-start.3
  7.2 0.0 copy-start.1
  7.2 0.0 reduce-scatter.2.cloned.1.call-start
  7.2 0.8 broadcast_multiply_fusion
  8.0 0.8 copy.19
  8.8 0.1 eq.34
  8.9 0.1 reshape.98
  9.0 0.1 copy.25
  9.1 0.1 mul.81
  9.2 18.0 %reduce-window.6 = s32[64,8,128]{2,1,0:T(8,128)S(1)} reduce-window(s32[64,8,128]{2,1,0:T(8,128)S(1)} %fusion.30, s32[]{:T(128)} %constant.41.clone.1), window={size=1x1x128 pad=0_0x0_0x127_0}, to_apply=%region_0.0 | reduce-window | flops 8323072 | bytes 524292 | tf_op jit(solution)/shard_map/reduce-window
  27.2 0.1 slice.28
  27.3 0.1 copy.21
  27.5 0.1 copy.22
  27.6 0.1 broadcast_add_fusion
  27.8 0.1 fusion.29
  27.9 4.3 %scatter_custom_fusion = s32[1024]{0:T(1024)S(1)} fusion(s32[1024]{0:T(1024)S(1)} %bitcast.75, s32[1024]{0:T(1024)S(1)} %iota.14, s32[]{:T(128)} %constant.58.clone.1), kind=kCustom, calls=%fused_computation.56 | custom fusion | bytes 4100 | tf_op jit(solution)/shard_map/scatter | solution.py:49
  32.2 0.0 copy-done.3
  32.2 0.1 copy.26
  32.3 0.1 mul.84
  32.4 0.0 copy-done.1
  32.4 0.1 broadcast_in_dim.33
  32.5 0.2 fusion.8
  32.7 0.1 concatenate.3
  32.8 3.9 %gather_fusion = bf16[1024,384]{1,0:T(8,128)(2,1)S(1)} fusion(bf16[1025,384]{1,0:T(8,128)(2,1)S(1)} %concatenate.3, s32[1024]{0:T(1024)S(1)} %fusion.31), kind=kCustom, calls=%fused_computation | custom fusion | bytes 1576960 | tf_op jit(solution)/shard_map/jit(_take)/gather | solution.py:55
  36.8 0.2 broadcast_select_fusion
  37.0 46.0 %all_to_all.10 = bf16[64,16,384]{2,1,0:T(8,128)(2,1)S(1)} all-to-all(bf16[64,16,384]{2,1,0:T(8,128)(2,1)S(1)} %broadcast_select_fusion), channel_id=1, replica_groups=mesh['node'=64,'local'=16] {'node'}, dimensions={0} | all-to-all | bytes 1572864 | tf_op jit(solution)/shard_map/all_to_all | solution.py:56
  83.0 0.0 copy-done
  83.0 2.6 convolution_convert_fusion
  85.6 0.0 reduce-scatter.2.cloned.1.call-update
  85.6 0.0 all-gather.3.cloned.1.call-start
  85.7 0.0 copy-start.4
  85.7 5.6 %copy.27 = bf16[1,64,16,2,1024]{4,2,1,3,0:T(8,128)(2,1)} copy(bf16[1,64,16,2,1024]{4,3,2,1,0:T(2,128)(2,1)} %param.12) | data formatting | bytes 8388608 | tf_op args[4]
  91.2 51.8 %reduce-scatter.2.cloned.1.call-done = bf16[64,1024]{1,0:T(8,128)(2,1)} async-done(((bf16[1024,1024]{1,0:T(8,128)(2,1)}), bf16[64,1024]{1,0:T(8,128)(2,1)}) %reduce-scatter.2.cloned.1.call-update) | async-done | bytes 131088 | tf_op jit(solution)/shard_map/reduce_scatter | solution.py:71
  143.1 1.9 fusion.26
  144.9 0.0 all-gather.3.cloned.1.call-update
  145.0 0.0 all-gather.5.cloned.1.call-start
  145.0 0.7 all-gather.5.cloned.1.call-update
  145.7 0.0 copy-start.5
  145.7 47.0 %all-gather.3.cloned.1.call-done = bf16[1024,1024]{1,0:T(8,128)(2,1)} async-done(((bf16[64,1024]{1,0:T(8,128)(2,1)}), bf16[1024,1024]{1,0:T(8,128)(2,1)}) %all-gather.3.cloned.1.call-update) | async-done | bytes 2097168 | tf_op jit(solution)/shard_map/all_gather | solution.py:78
  192.8 0.0 copy-done.4
  192.8 4.1 %fusion.15 = f32[1024,384]{1,0:T(8,128)} fusion(bf16[1024,1024]{1,0:T(8,128)(2,1)} %all-gather.3.cloned.1.call-done, bf16[1,384,1024]{2,1,0:T(8,128)(2,1)S(1)} %copy-done.4), kind=kOutput, calls=%fused_computation.22 | convolution fusion | flops 805306368 | bytes 4456448 | tf_op jit(solution)/shard_map/dot_general | solution.py:82
  196.9 43.2 %all-gather.5.cloned.1.call-done = bf16[1024,1024]{1,0:T(8,128)(2,1)} async-done(((bf16[64,1024]{1,0:T(8,128)(2,1)}), bf16[1024,1024]{1,0:T(8,128)(2,1)}) %all-gather.5.cloned.1.call-update) | async-done | bytes 2097168 | tf_op jit(solution)/shard_map/all_gather | solution.py:79
  240.1 0.0 copy-done.5
  240.1 4.2 %add_convert_fusion.1 = bf16[1024,384]{1,0:T(8,128)(2,1)} fusion(f32[1024,384]{1,0:T(8,128)} %fusion.15, bf16[1024,1024]{1,0:T(8,128)(2,1)} %all-gather.5.cloned.1.call-done, bf16[1,384,1024]{2,1,0:T(8,128)(2,1)S(1)} %copy-done.5), kind=kOutput, calls=%fused_computation.16 | convolution fusion | flops 806092800 | bytes 5242880 | tf_op jit(solution)/shard_map/dot_general | solution.py:83
  244.3 13.6 %all-to-all-start.1 = ((bf16[64,16,384]{2,1,0:T(8,128)(2,1)}), bf16[64,16,384]{2,1,0:T(8,128)(2,1)S(1)}, u32[]{:S(2)}, u32[]{:S(2)}) async-start(bf16[64,16,384]{2,1,0:T(8,128)(2,1)} %bitcast.14), calls=%async_computation.2 | async-start | bytes 1572864 | tf_op jit(solution)/shard_map/all_to_all | solution.py:88
  257.9 0.0 copy-start.2
  257.9 0.0 copy-start.6
  258.0 3.8 %fusion.9 = bf16[1024,384]{1,0:T(8,128)(2,1)S(1)} fusion(bf16[1024,384]{1,0:T(8,128)(2,1)S(1)} %bitcast.72, bf16[1024,2,1024]{2,0,1:T(8,128)(2,1)} %bitcast.68), kind=kOutput, calls=%fused_computation.17 | convolution fusion | flops 814088192 | bytes 5767168 | tf_op jit(solution)/shard_map/dot_general | solution.py:85
  261.8 7.5 %collective-permute-start = (bf16[1024,384]{1,0:T(8,128)(2,1)S(1)}, bf16[1024,384]{1,0:T(8,128)(2,1)S(1)}, u32[]{:S(2)}, u32[]{:S(2)}) collective-permute-start(bf16[1024,384]{1,0:T(8,128)(2,1)S(1)} %fusion.9), channel_id=1, source_target_pairs={{0,512},{512,0},{16,528},{528,16},{32,544},{544,32},{48,560},{560,... | collective-permute-start | bytes 2359304 | tf_op jit(solution)/shard_map/ppermute | solution.py:14
  269.3 0.1 reduce_sum.35
  269.4 0.0 copy-done.2
  269.5 0.1 copy.24
  269.6 0.0 copy-done.6
  269.6 0.6 fusion.34
  270.2 44.2 %collective-permute-done = bf16[1024,384]{1,0:T(8,128)(2,1)S(1)} collective-permute-done((bf16[1024,384]{1,0:T(8,128)(2,1)S(1)}, bf16[1024,384]{1,0:T(8,128)(2,1)S(1)}, u32[]{:S(2)}, u32[]{:S(2)}) %collective-permute-start) | collective-permute-done | bytes 786464 | tf_op jit(solution)/shard_map/ppermute | solution.py:14
  314.4 1.8 fusion.12
  316.1 0.0 all-to-all-done.1
  316.1 3.9 %gather_fusion.1 = bf16[1024,384]{1,0:T(8,128)(2,1)S(1)} fusion(bf16[1024,384]{1,0:T(8,128)(2,1)S(1)} %bitcast.66, s32[1024]{0:T(1024)S(1)} %broadcast_clamp_fusion), kind=kCustom, calls=%fused_computation.1 | custom fusion | bytes 1576960 | tf_op jit(solution)/shard_map/jit(_take)/gather | solution.py:91
  320.1 1.2 fusion.13
  (11 shorter events, 0.2 us)
Async XLA Ops:
  7.2 75.8 %copy-start = (bf16[1,1024,384]{2,1,0:T(8,128)(2,1)S(1)}, bf16[1,1024,384]{2,1,0:T(8,128)(2,1)}, u32[]{:S(2)}) copy-start(bf16[1,1024,384]{2,1,0:T(8,128)(2,1)} %param.15) | copy-start | bytes 2359300
  7.2 25.0 %copy-start.3 = (f32[128,8]{0,1:T(8,128)S(1)}, f32[128,8]{0,1:T(8,128)}, u32[]{:S(2)}) copy-start(f32[128,8]{0,1:T(8,128)} %param.9) | copy-start | bytes 12292
  7.2 25.2 %copy-start.1 = (bf16[128,384]{1,0:T(8,128)(2,1)S(1)}, bf16[128,384]{1,0:T(8,128)(2,1)}, u32[]{:S(2)}) copy-start(bf16[128,384]{1,0:T(8,128)(2,1)} %param.8) | copy-start | bytes 294916
  7.2 135.9 %reduce-scatter.2.cloned.1.call-start = ((), (), s32[]{:S(2)}) async-start(), calls=%async_computation.3 | async-start | bytes 2228224 | tf_op jit(solution)/shard_map/reduce_scatter | solution.py:71
  85.6 107.2 %all-gather.3.cloned.1.call-start = ((), (), s32[]{:S(2)}) async-start(), calls=%async_computation.4 | async-start | bytes 2228224 | tf_op jit(solution)/shard_map/all_gather | solution.py:78
  85.7 107.1 %copy-start.4 = (bf16[1,384,1024]{2,1,0:T(8,128)(2,1)S(1)}, bf16[1,384,1024]{2,1,0:T(8,128)(2,1)}, u32[]{:S(2)}) copy-start(bf16[1,384,1024]{2,1,0:T(8,128)(2,1)} %param.13) | copy-start | bytes 2359300
  145.0 95.1 %all-gather.5.cloned.1.call-start = ((), (), s32[]{:S(2)}) async-start(), calls=%async_computation.5 | async-start | bytes 2228224 | tf_op jit(solution)/shard_map/all_gather | solution.py:79
  145.7 94.4 %copy-start.5 = (bf16[1,384,1024]{2,1,0:T(8,128)(2,1)S(1)}, bf16[1,384,1024]{2,1,0:T(8,128)(2,1)}, u32[]{:S(2)}) copy-start(bf16[1,384,1024]{2,1,0:T(8,128)(2,1)} %param.14) | copy-start | bytes 2359300
  244.3 71.9 %all-to-all-start.1 = ((bf16[64,16,384]{2,1,0:T(8,128)(2,1)}), bf16[64,16,384]{2,1,0:T(8,128)(2,1)S(1)}, u32[]{:S(2)}, u32[]{:S(2)}) async-start(bf16[64,16,384]{2,1,0:T(8,128)(2,1)} %bitcast.14), calls=%async_computation.2 | async-start | bytes 1572864 | tf_op jit(solution)/shard_map/all_to_all | solution.py:88
  257.9 11.5 %copy-start.2 = (s32[128,8]{0,1:T(8,128)S(1)}, s32[128,8]{0,1:T(8,128)}, u32[]{:S(2)}) copy-start(s32[128,8]{0,1:T(8,128)} %param.10) | copy-start | bytes 12292
  257.9 11.6 %copy-start.6 = (s32[32]{0:T(128)S(1)}, s32[32]{0:T(128)}, u32[]{:S(2)}) copy-start(s32[32]{0:T(128)} %param.11) | copy-start | bytes 388
  261.8 52.6 %collective-permute-start = (bf16[1024,384]{1,0:T(8,128)(2,1)S(1)}, bf16[1024,384]{1,0:T(8,128)(2,1)S(1)}, u32[]{:S(2)}, u32[]{:S(2)}) collective-permute-start(bf16[1024,384]{1,0:T(8,128)(2,1)S(1)} %fusion.9), channel_id=1, source_target_pairs={{0,512},{512,0},{16,528},{528,16},{32,544},{544,32},{48,560},{560,... | collective-permute-start | bytes 2359304 | tf_op jit(solution)/shard_map/ppermute | solution.py:14
Sparse Core Ops, SparseCore 0:
  85.7 57.2 reduce-scatter.1
  145.8 46.9 all-gather.2
  196.0 43.9 all-gather.4
where the time goes:
time: 328 us
  waiting for transfers between devices  187 us (57%)
  blocking collectives  46 us (14%)
  other arithmetic  25 us (8%)
  starting transfers between devices  21.2 us (6%)
  local copies, waits for them, and re-layouts  19.9 us (6%)
  matrix products  14.8 us (5%)
  between operations  14 us (4%)
    reduce_scatter x1, waiting for transfers between devices, body(): lax.psum_scatter(partial_value.astype(jnp.bfloat16), 'local', scatter_dim...  51.8 us
    all_gather x1, waiting for transfers between devices, body(): lax.all_gather(dgate, 'local', axis=0, tiled=True)  47 us
    all_to_all x1, blocking collectives, body(): lax.all_to_all(outgoing.reshape(nodes, capacity, part_slice), 'node', spl...  46 us
    ppermute x1, waiting for transfers between devices, partner_2(): return lax.ppermute(block, axis, route)  44.2 us
    all_gather x1, waiting for transfers between devices, body(): lax.all_gather(dup, 'local', axis=0, tiled=True)  43.2 us
    another operation x3, other arithmetic  18.2 us
    all_to_all x1, starting transfers between devices, body(): lax.all_to_all(back.reshape(nodes, capacity, part_slice), 'node', split_a...  13.6 us
    ppermute x1, starting transfers between devices, partner_2(): return lax.ppermute(block, axis, route)  7.48 us
  transfers between devices with their start and end apart: 5, of which 4 were waited for; matrix products, arithmetic and copies ran while one was open for 5% of the time, Pallas kernels for 0%

commit v1 on v0

v1 whole, which is shorter than its diff:
```python
import functools

import jax
import jax.numpy as jnp
from jax import lax
from jax.experimental import pallas as pl
from jax.experimental.pallas import tpu as pltpu
from jax.sharding import PartitionSpec as P

MESH = pl.DeviceIdType.MESH
DEPTH = 8
F32 = jnp.float32
BF16 = jnp.bfloat16
NT = (((1,), (1,)), ((), ()))
PIECES = 2


def remote(src, dst, send, recv, **where):
    return pltpu.make_async_remote_copy(
        src_ref=src, dst_ref=dst, send_sem=send, recv_sem=recv, device_id=where, device_id_type=MESH
    )


def local_copy(src, dst, sem):
    return pltpu.make_async_copy(src, dst, sem)


def kernel(
    depth,
    grad_out, gate, routes, paired, pre_hbm, wg_hbm, wu_hbm, wd_hbm,
    gin, gdown,
    code, gates, onehot, rows_out, rows_in, pre, wg, wu, wd, fgate, fup, act, act_t,
    part, mate, long_out, long_in, short_out, short_in, dhid, back, homing, own, other,
    pre_sem, w_sem, rows_send, rows_recv, mate_send, mate_recv,
    long_send, long_recv, short_send, short_recv, own_send, own_recv,
    up_send, up_recv, down_send, down_recv, core_send, core_recv, home_send, home_recv,
):
    nodes, cap, feat = rows_out.shape
    slabs = part.shape[0]
    hidden = part.shape[3]
    share = part.shape[2]
    block = 2 * share
    group = nodes // slabs
    wide = nodes // depth
    tops, toks = routes.shape
    far, near = slabs // 2, slabs - 1 - slabs // 2
    size = share // PIECES

    me = lax.axis_index("node")
    at = lax.axis_index("local")
    my_x, my_z = me // depth, me % depth
    my_y, core = at // 2, at % 2
    sign = 1 - 2 * core
    mate_at = my_y * 2 + 1 - core

    def slab_of(step):
        return lax.rem(my_y + step + slabs, slabs)

    ahead = slab_of(sign) * 2 + core
    behind = slab_of(-sign) * 2 + core

    def offset_of(place):
        q, dz = place // depth, place % depth
        return lax.rem(q - dz + wide * depth, wide), dz

    def node_ahead(dx, dz):
        return lax.rem(my_x + dx, wide) * depth + lax.rem(my_z + dz, depth)

    def node_back(dx, dz):
        return lax.rem(my_x - dx + wide, wide) * depth + lax.rem(my_z - dz + depth, depth)

    def turn(i):
        k = far - (i + 1) // 2
        return lax.rem(my_y + jnp.where(i % 2 == 0, -k, k) + slabs, slabs)

    barrier = pltpu.get_barrier_semaphore()

    def greet(k, carry):
        pl.semaphore_signal(barrier, inc=1, device_id={"node": lax.rem(me + k, nodes)}, device_id_type=MESH)
        return carry

    lax.fori_loop(1, nodes, greet, 0)
    for other_at in (mate_at, ahead, behind):
        pl.semaphore_signal(barrier, inc=1, device_id={"local": other_at}, device_id_type=MESH)

    loads = [local_copy(a.at[0], b, w_sem.at[i]) for i, (a, b) in enumerate(((wd_hbm, wd), (wg_hbm, wg), (wu_hbm, wu)))]

    def load_pre(place, carry):
        dx, dz = offset_of(place)
        local_copy(pre_hbm.at[0, node_ahead(dx, dz)], pre.at[place], pre_sem.at[place // group]).start()
        return carry

    lax.fori_loop(0, nodes, load_pre, 0)
    for load in loads:
        load.start()

    slot_id = lax.broadcasted_iota(jnp.int32, (nodes, toks), 0)
    named = jnp.zeros((nodes, toks), F32)
    gate_of = jnp.zeros((nodes, toks), F32)
    for k in range(tops):
        hit = routes[k : k + 1, :] == slot_id
        named = jnp.where(hit, 1.0, named)
        gate_of = jnp.where(hit, gate[k : k + 1, :], gate_of)
    earlier = lax.broadcasted_iota(jnp.int32, (toks, toks), 0) < lax.broadcasted_iota(jnp.int32, (toks, toks), 1)
    rank = jnp.dot(named.astype(BF16), jnp.where(earlier, 1.0, 0.0).astype(BF16), preferred_element_type=F32)
    code[...] = jnp.where(named > 0.0, rank, -1.0)
    gates[...] = gate_of
    some = min(8, nodes)

    def fill(i, carry):
        slots = pl.ds(pl.multiple_of(i * some, some), some)
        want = lax.broadcasted_iota(jnp.int32, (some, cap, toks), 1).astype(F32)
        hit = code[slots, :][:, None, :] == want
        scale = jnp.sum(jnp.where(hit, gates[slots, :][:, None, :], 0.0), axis=2, keepdims=True)
        picks = jnp.where(hit, 1.0, 0.0).reshape(some * cap, toks).astype(BF16)
        onehot[pl.ds(pl.multiple_of(i * some * cap, some * cap), some * cap), :] = picks
        values = jnp.dot(picks, grad_out[...], preferred_element_type=F32)
        values = values.reshape(some, cap, feat) * scale
        rows_out[slots] = values.astype(BF16)
        return carry

    lax.fori_loop(0, nodes // some, fill, 0)

    pl.semaphore_wait(barrier, nodes - 1 + 3)

    def send_rows(n, carry):
        i, dz = n // depth, n % depth
        q = turn(i)
        dx = lax.rem(q - dz + wide * depth, wide)
        target = node_back(dx, dz)
        place = q * depth + dz

        @pl.when(target != me)
        def _():
            remote(rows_out.at[target], rows_in.at[place], rows_send, rows_recv.at[q], node=target).start()

        @pl.when(target == me)
        def _():
            local_copy(rows_out.at[target], rows_in.at[place], rows_recv.at[q]).start()

        return carry

    lax.fori_loop(0, nodes, send_rows, 0)

    def factors(q, carry):
        blocks = pl.ds(pl.multiple_of(q * group, group), group)
        local_copy(pre.at[blocks], pre.at[blocks], pre_sem.at[q]).wait()

        def one(i, carry):
            place = q * group + i
            both = pre[place].astype(F32)
            gval, uval = both[:, 0, :], both[:, 1, :]
            sigm = jax.nn.sigmoid(gval)
            silu = gval * sigm
            these = pl.ds(pl.multiple_of(place * cap, cap), cap)
            fgate[these, :] = uval * sigm * (1.0 + gval * (1.0 - sigm))
            fup[these, :] = silu
            act[pl.ds(pl.multiple_of(i * cap, cap), cap), :] = silu * uval
            return carry

        lax.fori_loop(0, group, one, 0)
        act_t[q] = act[...].T.astype(BF16)
        return carry

    lax.fori_loop(0, slabs, factors, 0)
    loads[0].wait()

    def product(i, carry):
        q = turn(i)
        blocks = pl.ds(pl.multiple_of(q * group, group), group)
        local_copy(rows_in.at[blocks], rows_in.at[blocks], rows_recv.at[q]).wait()
        value = lax.dot_general(rows_in[blocks].reshape(block, feat), wd[...], NT, preferred_element_type=F32)
        part[q] = value.astype(BF16).reshape(2, share, hidden)
        remote(part.at[q, 1 - core], mate.at[q], mate_send.at[q], mate_recv.at[q], local=mate_at).start()
        return carry

    def piece(p):
        return pl.ds(p * size, size)

    def mine(q, p):
        return part[q, core, piece(p), :].astype(F32) + mate[q, piece(p), :].astype(F32)

    def wait_mate(q):
        remote(part.at[q, 1 - core], mate.at[q], mate_send.at[q], mate_recv.at[q], local=mate_at).wait_recv()

    def along(kind, j, p):
        if kind == "long":
            return remote(
                long_out.at[j, piece(p)], long_in.at[j, piece(p)], long_send.at[j, p], long_recv.at[j, p], local=ahead
            )
        return remote(
            short_out.at[j, piece(p)], short_in.at[j, piece(p)], short_send.at[j, p], short_recv.at[j, p], local=behind
        )

    waited = set()

    def reduce_step(j):
        chains = [("long", far - j)] + ([("short", -(near - j))] if j < near else [])
        for _, step in chains:
            if step not in waited:
                wait_mate(slab_of(step * sign))
                waited.add(step)
        for p in range(PIECES):
            for kind, step in chains:
                total = mine(slab_of(step * sign), p)
                if j > 0:
                    along(kind, j - 1, p).wait_recv()
                    total = total + (long_in if kind == "long" else short_in)[j - 1, piece(p), :].astype(F32)
                (long_out if kind == "long" else short_out)[j, piece(p), :] = total.astype(BF16)
                along(kind, j, p).start()

    done = 0
    for j in range(far):
        need = min(slabs, 3 + 2 * j) if near > 0 else slabs
        lax.fori_loop(done, need, product, 0)
        done = need
        reduce_step(j)
    if done < slabs:
        lax.fori_loop(done, slabs, product, 0)

    wide_own = own.shape[1]

    def own_copy(i):
        return remote(
            own.at[i], other.at[i], own_send.at[i], own_recv.at[i], node=lax.rem(me + nodes // 2, nodes)
        )

    def own_piece(i, carry):
        these = pl.ds(pl.multiple_of(i * wide_own, wide_own), wide_own)
        value = jnp.zeros((wide_own, feat), F32)
        for q in range(slabs):
            value = value + jnp.dot(
                act_t[q, these, :], rows_in[q * group : (q + 1) * group].reshape(block, feat), preferred_element_type=F32
            )
        own[i] = value.astype(BF16)
        own_copy(i).start()
        return carry

    lax.fori_loop(0, own.shape[0], own_piece, 0)

    def hop(kind, k, p):
        q = slab_of(-k * sign if kind == "long" else k * sign)
        held = dhid.at[q, core, piece(p)]
        if kind == "long":
            return remote(held, held, up_send.at[k, p], up_recv.at[k, p], local=ahead)
        return remote(held, held, down_send.at[k, p], down_recv.at[k, p], local=behind)

    def cross(step, p):
        q = slab_of(step)
        held = dhid.at[q, core, piece(p)]
        return remote(held, held, core_send.at[q, p], core_recv.at[q, p], local=mate_at)

    wait_mate(my_y)
    for p in range(PIECES):
        total = mine(my_y, p)
        along("long", far - 1, p).wait_recv()
        total = total + long_in[far - 1, piece(p), :].astype(F32)
        if near > 0:
            along("short", near - 1, p).wait_recv()
            total = total + short_in[near - 1, piece(p), :].astype(F32)
        dhid[my_y, core, piece(p), :] = total.astype(BF16)
        hop("long", 0, p).start()
        if near > 0:
            hop("short", 0, p).start()
        cross(0, p).start()

    loads[1].wait()
    loads[2].wait()

    def send_back(n, q):
        place = q * depth + lax.rem(n + my_z, depth)
        dx, dz = offset_of(place)
        target = node_ahead(dx, dz)

        @pl.when(target != me)
        def _():
            remote(back.at[place], homing.at[me], home_send, home_recv.at[me // group], node=target).start()

        @pl.when(target == me)
        def _():
            local_copy(back.at[place], homing.at[me], home_recv.at[me // group]).start()

        return q

    def rows_back(q):
        for p in range(PIECES):
            held = dhid.at[q, 1 - core, piece(p)]
            remote(held, held, core_send.at[q, p], core_recv.at[q, p], local=mate_at).wait_recv()
        these = pl.ds(pl.multiple_of(q * block, block), block)
        value = dhid[q].reshape(block, hidden).astype(F32)
        dgate = (value * fgate[these, :]).astype(BF16)
        dup = (value * fup[these, :]).astype(BF16)
        result = lax.dot_general(dgate, wg[...], NT, preferred_element_type=F32)
        result = result + lax.dot_general(dup, wu[...], NT, preferred_element_type=F32)
        back[pl.ds(pl.multiple_of(q * group, group), group)] = result.astype(BF16).reshape(group, cap, feat)
        lax.fori_loop(0, group, send_back, q)

    def rows_back_pair(k, count):
        def body(i, carry):
            rows_back(slab_of(jnp.where(i == 0, -k, k)))
            return carry

        lax.fori_loop(0, count, body, 0)

    for k in range(1, far + 1):
        for p in range(PIECES):
            hop("long", k - 1, p).wait_recv()
            if k < far:
                hop("long", k, p).start()
            cross(-k * sign, p).start()
            if k <= near:
                hop("short", k - 1, p).wait_recv()
                if k < near:
                    hop("short", k, p).start()
                cross(k * sign, p).start()
        rows_back_pair(k - 1, 1 if k == 1 else 2)
    rows_back_pair(far, 1)

    total = jnp.zeros((toks, feat), F32)
    for g in range(slabs):
        blocks = pl.ds(g * group, group)
        local_copy(homing.at[blocks], homing.at[blocks], home_recv.at[g]).wait()
        total = total + lax.dot_general(
            onehot[g * block : (g + 1) * block, :],
            homing[g * group : (g + 1) * group].reshape(block, feat),
            (((0,), (0,)), ((), ())),
            preferred_element_type=F32,
        )
    gin[...] = total.astype(BF16)

    half = nodes // 2
    pair_id = lax.broadcasted_iota(jnp.int32, paired.shape, 1)
    flag = jnp.sum(jnp.where(pair_id == lax.rem(me, half), paired[...].astype(F32), 0.0), axis=1, keepdims=True)

    def finish(i, carry):
        own_copy(i).wait_recv()
        value = own[i].astype(F32) + flag * other[i].astype(F32)
        gdown[pl.ds(pl.multiple_of(i * wide_own, wide_own), wide_own), :] = value.astype(BF16)
        return carry

    lax.fori_loop(0, own.shape[0], finish, 0)

    rest = rows_out.at[pl.ds(0, nodes - 1)]
    local_copy(rest, rest, rows_send).wait()
    local_copy(rest, rest, home_send).wait()
    for q in range(slabs):
        remote(part.at[q, 1 - core], mate.at[q], mate_send.at[q], mate_recv.at[q], local=mate_at).wait_send()
        for p in range(PIECES):
            held = dhid.at[q, core, piece(p)]
            remote(held, held, core_send.at[q, p], core_recv.at[q, p], local=mate_at).wait_send()
    for p in range(PIECES):
        for j in range(far):
            along("long", j, p).wait_send()
            hop("long", j, p).wait_send()
        for j in range(near):
            along("short", j, p).wait_send()
            hop("short", j, p).wait_send()
    for i in range(own.shape[0]):
        own_copy(i).wait_send()


def body(depth, grad_out, gate_prob, routes, paired, saved_pre, w_gate, w_up, w_down):
    toks, feat = grad_out.shape
    nodes, cap, hidden = saved_pre.shape[1], saved_pre.shape[2], saved_pre.shape[4]
    slabs = lax.axis_size("local") // 2
    rows = nodes * cap
    block = rows // slabs
    share = block // 2
    group = nodes // slabs
    far = slabs // 2
    near = slabs - 1 - far
    slots = max(near, 1)
    pieces_own = max(1, hidden // 128)
    vmem, dma = pltpu.VMEM, pltpu.SemaphoreType.DMA
    scratch = [
        vmem((nodes, toks), F32),
        vmem((nodes, toks), F32),
        vmem((rows, toks), BF16),
        vmem((nodes, cap, feat), BF16),
        vmem((nodes, cap, feat), BF16),
        vmem((nodes, cap, 2, hidden), BF16),
        vmem((feat, hidden), BF16),
        vmem((feat, hidden), BF16),
        vmem((hidden, feat), BF16),
        vmem((rows, hidden), F32),
        vmem((rows, hidden), F32),
        vmem((block, hidden), F32),
        vmem((slabs, hidden, block), BF16),
        vmem((slabs, 2, share, hidden), BF16),
        vmem((slabs, share, hidden), BF16),
        vmem((far, share, hidden), BF16),
        vmem((far, share, hidden), BF16),
        vmem((slots, share, hidden), BF16),
        vmem((slots, share, hidden), BF16),
        vmem((slabs, 2, share, hidden), BF16),
        vmem((nodes, cap, feat), BF16),
        vmem((nodes, cap, feat), BF16),
        vmem((pieces_own, hidden // pieces_own, feat), BF16),
        vmem((pieces_own, hidden // pieces_own, feat), BF16),
        dma((slabs,)),
        dma((3,)),
        dma,
        dma((slabs,)),
        dma((slabs,)),
        dma((slabs,)),
        dma((far, PIECES)),
        dma((far, PIECES)),
        dma((slots, PIECES)),
        dma((slots, PIECES)),
        dma((pieces_own,)),
        dma((pieces_own,)),
        dma((far, PIECES)),
        dma((far, PIECES)),
        dma((slots, PIECES)),
        dma((slots, PIECES)),
        dma((slabs, PIECES)),
        dma((slabs, PIECES)),
        dma,
        dma((slabs,)),
    ]
    whole = pl.BlockSpec(memory_space=pltpu.VMEM)
    stay = pl.BlockSpec(memory_space=pl.ANY)
    grad_in, grad_down = pl.pallas_call(
        functools.partial(kernel, depth),
        out_shape=(
            jax.ShapeDtypeStruct((toks, feat), BF16),
            jax.ShapeDtypeStruct((hidden, feat), BF16),
        ),
        in_specs=[whole] * 4 + [stay] * 4,
        out_specs=(whole, whole),
        scratch_shapes=scratch,
        compiler_params=pltpu.CompilerParams(
            collective_id=0, has_side_effects=True, vmem_limit_bytes=60 * 1024 * 1024
        ),
        name="expert_backward",
    )(grad_out, gate_prob.T, routes.T, paired[None, :], saved_pre, w_gate, w_up, w_down)
    return grad_in, grad_down[None]


def solution(mesh, depth=DEPTH):
    in_specs = (
        P("node", "local"),
        P("node", None),
        P("node", None),
        P(),
        P("node", None, None, None, None),
        P("node", "local", None),
        P("node", "local", None),
        P("node", None, "local"),
    )
    out_specs = (P("node", "local"), P("node", None, "local"))
    return jax.shard_map(
        functools.partial(body, depth), mesh=mesh, in_specs=in_specs, out_specs=out_specs, check_vma=False
    )
```

time: 328 us -> 113 us (0.34)
  the two profiles are of different devices: /device:TPU:16 before, /device:TPU:1 now
where the time goes in v1:
time: 113 us; the launch traced here: 112 us
  Pallas kernels  108 us (96%)
  local copies, waits for them, and re-layouts  3.63 us (3%)
    pallas_call x1, Pallas kernels, body(): pl.pallas_call(functools.partial(kernel, depth), out_shape=(jax.ShapeDtyp...  108 us
    unnamed x2, local copies, waits for them, and re-layouts  3.63 us

profile of v1, /device:TPU:1, one launch (start us, length us, event | category | flops | bytes accessed | tf_op | source)
XLA Modules:
  0.0 112.5 jit_solution(16127647478996743541)
XLA Ops:
  0.6 108.2 %expert_backward.1 = (bf16[128,384]{1,0:T(8,128)(2,1)}, bf16[1024,384]{1,0:T(8,128)(2,1)}) custom-call(bf16[128,384]{1,0:T(8,128)(2,1)} %grad_out.1, f32[8,128]{1,0:T(8,128)} %bitcast.5, s32[8,128]{1,0:T(8,128)} %bitcast.6, s32[1,32]{1,0:T(1,128)} %bitcast.7, bf16[1,64,16,2,1024]{4,3,2,1,0:T(2,128)(2,1)} %pre_hbm.1, bf16[1,384,1024]{2,1,0:T(8,128)(2,1)} %wg_hbm.1, ...), custom_call_target="tpu_custom_call" | custom-call | tf_op jit(solution)/shard_map/expert_backward/pallas_call | solution.py:423
  108.8 1.5 %copy.12 = bf16[128,384]{1,0:T(8,128)(2,1)} copy(bf16[128,384]{1,0:T(8,128)(2,1)} %get-tuple-element.8) | data formatting | bytes 196608
  110.4 2.1 %copy.13 = bf16[1,1024,384]{2,1,0:T(8,128)(2,1)} copy(bf16[1,1024,384]{2,1,0:T(8,128)(2,1)} %bitcast.4) | data formatting | bytes 1572864

commit v2 on v1

--- a/solution.py
+++ b/solution.py
@@ -30,9 +30,10 @@
     grad_out, gate, routes, paired, pre_hbm, wg_hbm, wu_hbm, wd_hbm,
     gin, gdown,
     code, gates, onehot, rows_out, rows_in, pre, wg, wu, wd, fgate, fup, act, act_t,
-    part, mate, long_out, long_in, short_out, short_in, dhid, back, homing, own, other,
+    part, mate, long_out, long_in, short_out, short_in, dhid, back, homing, own, rows_two, act_out, act_two,
     pre_sem, w_sem, rows_send, rows_recv, mate_send, mate_recv,
-    long_send, long_recv, short_send, short_recv, own_send, own_recv,
+    long_send, long_recv, short_send, short_recv, two_send, two_recv, twin_send, twin_recv,
+    act_up_send, act_up_recv, act_down_send, act_down_recv, act_core_send, act_core_recv,
     up_send, up_recv, down_send, down_recv, core_send, core_recv, home_send, home_recv,
 ):
     nodes, cap, feat = rows_out.shape
@@ -52,6 +53,7 @@
     my_y, core = at // 2, at % 2
     sign = 1 - 2 * core
     mate_at = my_y * 2 + 1 - core
+    twin = lax.rem(me + nodes // 2, nodes)
 
     def slab_of(step):
         return lax.rem(my_y + step + slabs, slabs)
@@ -85,7 +87,8 @@
 
     loads = [local_copy(a.at[0], b, w_sem.at[i]) for i, (a, b) in enumerate(((wd_hbm, wd), (wg_hbm, wg), (wu_hbm, wu)))]
 
-    def load_pre(place, carry):
+    def load_pre(n, carry):
+        place = lax.rem(n + my_y * group, nodes)
         dx, dz = offset_of(place)
         local_copy(pre_hbm.at[0, node_ahead(dx, dz)], pre.at[place], pre_sem.at[place // group]).start()
         return carry
@@ -121,28 +124,8 @@
 
     lax.fori_loop(0, nodes // some, fill, 0)
 
-    pl.semaphore_wait(barrier, nodes - 1 + 3)
-
-    def send_rows(n, carry):
-        i, dz = n // depth, n % depth
-        q = turn(i)
-        dx = lax.rem(q - dz + wide * depth, wide)
-        target = node_back(dx, dz)
-        place = q * depth + dz
-
-        @pl.when(target != me)
-        def _():
-            remote(rows_out.at[target], rows_in.at[place], rows_send, rows_recv.at[q], node=target).start()
-
-        @pl.when(target == me)
-        def _():
-            local_copy(rows_out.at[target], rows_in.at[place], rows_recv.at[q]).start()
-
-        return carry
-
-    lax.fori_loop(0, nodes, send_rows, 0)
-
-    def factors(q, carry):
+    def factors(n, carry):
+        q = lax.rem(my_y + n, slabs)
         blocks = pl.ds(pl.multiple_of(q * group, group), group)
         local_copy(pre.at[blocks], pre.at[blocks], pre_sem.at[q]).wait()
 
@@ -162,7 +145,55 @@
         act_t[q] = act[...].T.astype(BF16)
         return carry
 
-    lax.fori_loop(0, slabs, factors, 0)
+    factors(0, 0)
+    act_out[...] = act[pl.ds(pl.multiple_of(core * share, share), share), :].astype(BF16)
+
+    pl.semaphore_wait(barrier, nodes - 1 + 3)
+
+    def send_rows(n, carry):
+        i, dz = n // depth, n % depth
+        q = turn(i)
+        dx = lax.rem(q - dz + wide * depth, wide)
+        target = node_back(dx, dz)
+        place = q * depth + dz
+
+        @pl.when(target != me)
+        def _():
+            remote(rows_out.at[target], rows_in.at[place], rows_send, rows_recv.at[q], node=target).start()
+
+        @pl.when(target == me)
+        def _():
+            local_copy(rows_out.at[target], rows_in.at[place], rows_recv.at[q]).start()
+
+        return carry
+
+    def send_twin(n, carry):
+        i, dz = n // depth, n % depth
+        q = turn(i)
+        dx = lax.rem(q - dz + wide * depth, wide)
+        slot = node_back(dx, dz)
+        target = lax.rem(slot + nodes // 2, nodes)
+        place = q * depth + dz
+
+        @pl.when(target != me)
+        def _():
+            remote(rows_out.at[slot], rows_two.at[place], two_send, two_recv, node=target).start()
+
+        @pl.when(target == me)
+        def _():
+            local_copy(rows_out.at[slot], rows_two.at[place], two_recv).start()
+
+        return carry
+
+    def to_twin():
+        return remote(act_out, act_two.at[my_y, core], twin_send, twin_recv, node=twin)
+
+    first = min(slabs, 3) * group
+    lax.fori_loop(0, first, send_rows, 0)
+    to_twin().start()
+    lax.fori_loop(first, nodes, send_rows, 0)
+
+    lax.fori_loop(1, slabs, factors, 0)
     loads[0].wait()
 
     def product(i, carry):
@@ -209,46 +240,71 @@
                 (long_out if kind == "long" else short_out)[j, piece(p), :] = total.astype(BF16)
                 along(kind, j, p).start()
 
-    done = 0
-    for j in range(far):
-        need = min(slabs, 3 + 2 * j) if near > 0 else slabs
-        lax.fori_loop(done, need, product, 0)
-        done = need
-        reduce_step(j)
-    if done < slabs:
-        lax.fori_loop(done, slabs, product, 0)
+    def hop(array, kind, k, p):
+        q = slab_of(-k * sign if kind == "long" else k * sign)
+        held = array.at[q, core, piece(p)]
+        up, up_in, down, down_in = (
+            (up_send, up_recv, down_send, down_recv)
+            if array is dhid
+            else (act_up_send, act_up_recv, act_down_send, act_down_recv)
+        )
+        if kind == "long":
+            return remote(held, held, up.at[k, p], up_in.at[k, p], local=ahead)
+        return remote(held, held, down.at[k, p], down_in.at[k, p], local=behind)
+
+    def cross(array, q, side, p):
+        held = array.at[q, side, piece(p)]
+        out, into = (core_send, core_recv) if array is dhid else (act_core_send, act_core_recv)
+        return remote(held, held, out.at[q, p], into.at[q, p], local=mate_at)
+
+    def spread(array, k):
+        for p in range(PIECES):
+            if k > 0:
+                hop(array, "long", k - 1, p).wait_recv()
+            if k < far:
+                hop(array, "long", k, p).start()
+            cross(array, slab_of(-k * sign), core, p).start()
+            if 0 < k <= near:
+                hop(array, "short", k - 1, p).wait_recv()
+            if k < near:
+                hop(array, "short", k, p).start()
+            if 0 < k <= near:
+                cross(array, slab_of(k * sign), core, p).start()
 
     wide_own = own.shape[1]
-
-    def own_copy(i):
-        return remote(
-            own.at[i], other.at[i], own_send.at[i], own_recv.at[i], node=lax.rem(me + nodes // 2, nodes)
-        )
-
-    def own_piece(i, carry):
+    count = own.shape[0]
+
+    def gradient(i, rows):
         these = pl.ds(pl.multiple_of(i * wide_own, wide_own), wide_own)
         value = jnp.zeros((wide_own, feat), F32)
         for q in range(slabs):
             value = value + jnp.dot(
-                act_t[q, these, :], rows_in[q * group : (q + 1) * group].reshape(block, feat), preferred_element_type=F32
+                act_t[q, these, :], rows[q * group : (q + 1) * group].reshape(block, feat), preferred_element_type=F32
             )
-        own[i] = value.astype(BF16)
-        own_copy(i).start()
-        return carry
-
-    lax.fori_loop(0, own.shape[0], own_piece, 0)
-
-    def hop(kind, k, p):
-        q = slab_of(-k * sign if kind == "long" else k * sign)
-        held = dhid.at[q, core, piece(p)]
-        if kind == "long":
-            return remote(held, held, up_send.at[k, p], up_recv.at[k, p], local=ahead)
-        return remote(held, held, down_send.at[k, p], down_recv.at[k, p], local=behind)
-
-    def cross(step, p):
-        q = slab_of(step)
-        held = dhid.at[q, core, piece(p)]
-        return remote(held, held, core_send.at[q, p], core_recv.at[q, p], local=mate_at)
+        return value.astype(BF16)
+
+    def own_piece(i, carry):
+        own[i] = gradient(i, rows_in)
+        return carry
+
+    lax.fori_loop(0, min(slabs, 3), product, 0)
+    reduce_step(0)
+    lax.fori_loop(min(slabs, 3), min(slabs, 5), product, 0)
+    if far > 1:
+        reduce_step(1)
+    lax.fori_loop(0, nodes, send_twin, 0)
+    to_twin().wait_recv()
+    spread(act_two, 0)
+    lax.fori_loop(min(slabs, 5), slabs, product, 0)
+    if far > 2:
+        reduce_step(2)
+    lax.fori_loop(0, count // 2, own_piece, 0)
+    spread(act_two, 1)
+    for j in range(3, far):
+        reduce_step(j)
+    lax.fori_loop(count // 2, count, own_piece, 0)
+    if far > 1:
+        spread(act_two, 2)
 
     wait_mate(my_y)
     for p in range(PIECES):
@@ -259,11 +315,8 @@
             along("short", near - 1, p).wait_recv()
             total = total + short_in[near - 1, piece(p), :].astype(F32)
         dhid[my_y, core, piece(p), :] = total.astype(BF16)
-        hop("long", 0, p).start()
-        if near > 0:
-            hop("short", 0, p).start()
-        cross(0, p).start()
-
+
+    spread(dhid, 0)
     loads[1].wait()
     loads[2].wait()
 
@@ -284,8 +337,7 @@
 
     def rows_back(q):
         for p in range(PIECES):
-            held = dhid.at[q, 1 - core, piece(p)]
-            remote(held, held, core_send.at[q, p], core_recv.at[q, p], local=mate_at).wait_recv()
+            cross(dhid, q, 1 - core, p).wait_recv()
         these = pl.ds(pl.multiple_of(q * block, block), block)
         value = dhid[q].reshape(block, hidden).astype(F32)
         dgate = (value * fgate[these, :]).astype(BF16)
@@ -303,18 +355,31 @@
         lax.fori_loop(0, count, body, 0)
 
     for k in range(1, far + 1):
+        spread(dhid, k)
+        rows_back_pair(k - 1, 1 if k == 1 else 2)
+        if 2 < k + 2 <= far:
+            spread(act_two, k + 2)
+    rows_back_pair(far, 1)
+
+    half = nodes // 2
+    pair_id = lax.broadcasted_iota(jnp.int32, paired.shape, 1)
+    flag = jnp.sum(jnp.where(pair_id == lax.rem(me, half), paired[...].astype(F32), 0.0), axis=1, keepdims=True)
+
+    def turned(q, carry):
         for p in range(PIECES):
-            hop("long", k - 1, p).wait_recv()
-            if k < far:
-                hop("long", k, p).start()
-            cross(-k * sign, p).start()
-            if k <= near:
-                hop("short", k - 1, p).wait_recv()
-                if k < near:
-                    hop("short", k, p).start()
-                cross(k * sign, p).start()
-        rows_back_pair(k - 1, 1 if k == 1 else 2)
-    rows_back_pair(far, 1)
+            cross(act_two, q, 1 - core, p).wait_recv()
+        act_t[q] = act_two[q].reshape(block, hidden).astype(F32).T.astype(BF16)
+        return carry
+
+    lax.fori_loop(0, slabs, turned, 0)
+    local_copy(rows_two, rows_two, two_recv).wait()
+
+    def finish(i, carry):
+        value = own[i].astype(F32) + flag * gradient(i, rows_two).astype(F32)
+        gdown[pl.ds(pl.multiple_of(i * wide_own, wide_own), wide_own), :] = value.astype(BF16)
+        return carry
+
+    lax.fori_loop(0, count, finish, 0)
 
     total = jnp.zeros((toks, feat), F32)
     for g in range(slabs):
@@ -328,35 +393,25 @@
         )
     gin[...] = total.astype(BF16)
 
-    half = nodes // 2
-    pair_id = lax.broadcasted_iota(jnp.int32, paired.shape, 1)
-    flag = jnp.sum(jnp.where(pair_id == lax.rem(me, half), paired[...].astype(F32), 0.0), axis=1, keepdims=True)
-
-    def finish(i, carry):
-        own_copy(i).wait_recv()
-        value = own[i].astype(F32) + flag * other[i].astype(F32)
-        gdown[pl.ds(pl.multiple_of(i * wide_own, wide_own), wide_own), :] = value.astype(BF16)
-        return carry
-
-    lax.fori_loop(0, own.shape[0], finish, 0)
-
     rest = rows_out.at[pl.ds(0, nodes - 1)]
     local_copy(rest, rest, rows_send).wait()
     local_copy(rest, rest, home_send).wait()
+    local_copy(rest, rest, two_send).wait()
+    to_twin().wait_send()
     for q in range(slabs):
         remote(part.at[q, 1 - core], mate.at[q], mate_send.at[q], mate_recv.at[q], local=mate_at).wait_send()
         for p in range(PIECES):
-            held = dhid.at[q, core, piece(p)]
-            remote(held, held, core_send.at[q, p], core_recv.at[q, p], local=mate_at).wait_send()
+            for array in (dhid, act_two):
+                cross(array, q, core, p).wait_send()
     for p in range(PIECES):
         for j in range(far):
             along("long", j, p).wait_send()
-            hop("long", j, p).wait_send()
+            for array in (dhid, act_two):
+                hop(array, "long", j, p).wait_send()
         for j in range(near):
             along("short", j, p).wait_send()
-            hop("short", j, p).wait_send()
-    for i in range(own.shape[0]):
-        own_copy(i).wait_send()
+            for array in (dhid, act_two):
+                hop(array, "short", j, p).wait_send()
 
 
 def body(depth, grad_out, gate_prob, routes, paired, saved_pre, w_gate, w_up, w_down):
@@ -396,7 +451,9 @@
         vmem((nodes, cap, feat), BF16),
         vmem((nodes, cap, feat), BF16),
         vmem((pieces_own, hidden // pieces_own, feat), BF16),
-        vmem((pieces_own, hidden // pieces_own, feat), BF16),
+        vmem((nodes, cap, feat), BF16),
+        vmem((share, hidden), BF16),
+        vmem((slabs, 2, share, hidden), BF16),
         dma((slabs,)),
         dma((3,)),
         dma,
@@ -407,8 +464,16 @@
         dma((far, PIECES)),
         dma((slots, PIECES)),
         dma((slots, PIECES)),
-        dma((pieces_own,)),
-        dma((pieces_own,)),
+        dma,
+        dma,
+        dma,
+        dma,
+        dma((far, PIECES)),
+        dma((far, PIECES)),
+        dma((slots, PIECES)),
+        dma((slots, PIECES)),
+        dma((slabs, PIECES)),
+        dma((slabs, PIECES)),
         dma((far, PIECES)),
         dma((far, PIECES)),
         dma((slots, PIECES)),
@@ -423,8 +488,8 @@
     grad_in, grad_down = pl.pallas_call(
         functools.partial(kernel, depth),
         out_shape=(
-            jax.ShapeDtypeStruct((toks, feat), BF16),
-            jax.ShapeDtypeStruct((hidden, feat), BF16),
+            pltpu.VMEM((toks, feat), BF16),
+            pltpu.VMEM((hidden, feat), BF16),
         ),
         in_specs=[whole] * 4 + [stay] * 4,
         out_specs=(whole, whole),

time: 113 us -> 98.5 us (0.87)
  Pallas kernels: 108 us -> 96.2 us
  local copies, waits for them, and re-layouts: 3.63 us -> 1.52 us
    pallas_call x1, Pallas kernels: 108 us -> 96.2 us  [body(): pl.pallas_call(functools.partial(kernel, depth), out_shape=(pltpu.VMEM((t...]
    unnamed x2, local copies, waits for them, and re-layouts: 3.63 us -> 1.52 us
where the time goes in v2:
time: 98.5 us; the launch traced here: 98.4 us
  Pallas kernels  96.2 us (98%)
  local copies, waits for them, and re-layouts  1.52 us (2%)
    pallas_call x1, Pallas kernels, body(): pl.pallas_call(functools.partial(kernel, depth), out_shape=(pltpu.VMEM((t...  96.2 us

profile of v2, /device:TPU:1, one launch (start us, length us, event | category | flops | bytes accessed | tf_op | source)
XLA Modules:
  0.0 98.4 jit_solution(9151057494806901827)
XLA Ops:
  0.6 96.2 %expert_backward.1 = (bf16[128,384]{1,0:T(8,128)(2,1)S(1)}, bf16[1024,384]{1,0:T(8,128)(2,1)S(1)}) custom-call(bf16[128,384]{1,0:T(8,128)(2,1)} %grad_out.1, f32[8,128]{1,0:T(8,128)} %bitcast.5, s32[8,128]{1,0:T(8,128)} %bitcast.6, s32[1,32]{1,0:T(1,128)} %bitcast.7, bf16[1,64,16,2,1024]{4,3,2,1,0:T(2,128)(2,1)} %pre_hbm.1, bf16[1,384,1024]{2,1,0:T(8,128)(2,1)} %wg_hbm.1, ...), custom_call_target="tpu_custom_call" | custom-call | tf_op jit(solution)/shard_map/expert_backward/pallas_call | solution.py:488
  96.8 0.6 copy.12
  97.5 0.9 copy.13

commit v3 on v2

--- a/solution.py
+++ b/solution.py
@@ -12,7 +12,7 @@
 F32 = jnp.float32
 BF16 = jnp.bfloat16
 NT = (((1,), (1,)), ((), ()))
-PIECES = 2
+PIECES = 4
 
 
 def remote(src, dst, send, recv, **where):
@@ -145,9 +145,6 @@
         act_t[q] = act[...].T.astype(BF16)
         return carry
 
-    factors(0, 0)
-    act_out[...] = act[pl.ds(pl.multiple_of(core * share, share), share), :].astype(BF16)
-
     pl.semaphore_wait(barrier, nodes - 1 + 3)
 
     def send_rows(n, carry):
@@ -188,10 +185,9 @@
     def to_twin():
         return remote(act_out, act_two.at[my_y, core], twin_send, twin_recv, node=twin)
 
-    first = min(slabs, 3) * group
-    lax.fori_loop(0, first, send_rows, 0)
-    to_twin().start()
-    lax.fori_loop(first, nodes, send_rows, 0)
+    lax.fori_loop(0, nodes, send_rows, 0)
+    factors(0, 0)
+    act_out[...] = act[pl.ds(pl.multiple_of(core * share, share), share), :].astype(BF16)
 
     lax.fori_loop(1, slabs, factors, 0)
     loads[0].wait()
@@ -292,19 +288,15 @@
     lax.fori_loop(min(slabs, 3), min(slabs, 5), product, 0)
     if far > 1:
         reduce_step(1)
+    to_twin().start()
     lax.fori_loop(0, nodes, send_twin, 0)
-    to_twin().wait_recv()
-    spread(act_two, 0)
     lax.fori_loop(min(slabs, 5), slabs, product, 0)
     if far > 2:
         reduce_step(2)
     lax.fori_loop(0, count // 2, own_piece, 0)
-    spread(act_two, 1)
     for j in range(3, far):
         reduce_step(j)
     lax.fori_loop(count // 2, count, own_piece, 0)
-    if far > 1:
-        spread(act_two, 2)
 
     wait_mate(my_y)
     for p in range(PIECES):
@@ -354,12 +346,21 @@
 
         lax.fori_loop(0, count, body, 0)
 
+    later = 0
     for k in range(1, far + 1):
         spread(dhid, k)
+        if k >= far - 1:
+            if later == 0:
+                to_twin().wait_recv()
+            spread(act_two, later)
+            later += 1
         rows_back_pair(k - 1, 1 if k == 1 else 2)
-        if 2 < k + 2 <= far:
-            spread(act_two, k + 2)
+    if later <= far:
+        spread(act_two, later)
+        later += 1
     rows_back_pair(far, 1)
+    for k in range(later, far + 1):
+        spread(act_two, k)
 
     half = nodes // 2
     pair_id = lax.broadcasted_iota(jnp.int32, paired.shape, 1)

time: 98.5 us -> 96.7 us (0.982)
  Pallas kernels: 96.2 us -> 94.3 us
    pallas_call x1, Pallas kernels: 96.2 us -> 94.3 us  [body(): pl.pallas_call(functools.partial(kernel, depth), out_shape=(pltpu.VMEM((t...]
where the time goes in v3:
time: 96.7 us; the launch traced here: 96.5 us
  Pallas kernels  94.3 us (98%)
  local copies, waits for them, and re-layouts  1.52 us (2%)
    pallas_call x1, Pallas kernels, body(): pl.pallas_call(functools.partial(kernel, depth), out_shape=(pltpu.VMEM((t...  94.3 us

profile of v3, /device:TPU:1, one launch (start us, length us, event | category | flops | bytes accessed | tf_op | source)
XLA Modules:
  0.0 96.5 jit_solution(1076398781819932907)
XLA Ops:
  0.6 94.3 %expert_backward.1 = (bf16[128,384]{1,0:T(8,128)(2,1)S(1)}, bf16[1024,384]{1,0:T(8,128)(2,1)S(1)}) custom-call(bf16[128,384]{1,0:T(8,128)(2,1)} %grad_out.1, f32[8,128]{1,0:T(8,128)} %bitcast.5, s32[8,128]{1,0:T(8,128)} %bitcast.6, s32[1,32]{1,0:T(1,128)} %bitcast.7, bf16[1,64,16,2,1024]{4,3,2,1,0:T(2,128)(2,1)} %pre_hbm.1, bf16[1,384,1024]{2,1,0:T(8,128)(2,1)} %wg_hbm.1, ...), custom_call_target="tpu_custom_call" | custom-call | tf_op jit(solution)/shard_map/expert_backward/pallas_call | solution.py:489
  95.0 0.6 copy.12
  95.6 0.9 copy.13
